TPU v7x, 32 devices: a whole 2x2x4 slice. The times are simulated.
32 devices in a mesh: tm: 2 (over y), pts: 16 (over z, x, core).
Axes of the slice: x: 2, y: 2, z: 4, core: 2. Of those that a mesh axis runs over, the one named last changes fastest.
Arguments:
- precip: float32 [512, 16384], P('tm', 'pts'), may hold values from -150 to 300, as said below
- thresholds: float32 [64], replicated, may hold values from -1 to 5
- bin_index: int32 [16384], P('pts'), may hold values from 0 to 63
- test_matrix: float32 [512, 256], P('tm'), may hold values from -0.25 to 0.25
Outputs:
- basis: float32 [16384, 256], P(('pts', 'tm'))
- factor: float32 [256, 256], replicated
Inputs may be any that keep to these rules, and one draw needn't show every extreme that they name: `precip`: precipitation records.
All inputs are finite; a program needn't handle non-finite values.
Results may differ from a plain program's by a relative error of at most 0.0003.
Values sent between devices are 32-bit elements; how exact they have to be, the bound alone decides.
No kernel may reach another device: no remote copies, remote signals or barrier semaphores. Data moves between devices by JAX's collectives and lax.ppermute only.
A program may use at most 64 MiB of HBM per device.

v0:
```python
import math
import jax
import jax.numpy as jnp
from jax import lax
from jax.sharding import PartitionSpec as P

HARM = 8
year_days = 365.25


def harmonic_table(day_number):
    phase_base = day_number.astype(jnp.float32)
    columns = [jnp.ones_like(phase_base)]
    for order in range(1, HARM + 1):
        phase = 2.0 * math.pi * order / year_days * phase_base
        columns.append(jnp.cos(phase))
        columns.append(jnp.sin(phase))
    return jnp.stack(columns, 0)


def normal_solve(factor_low, values):
    forward = lax.linalg.triangular_solve(factor_low, values, left_side=True, lower=True)
    return lax.linalg.triangular_solve(
        factor_low, forward, left_side=True, lower=True, transpose_a=True
    )


AXES = ("tm", "pts")


def swap(value, bit):
    total = lax.axis_size("tm") * lax.axis_size("pts")
    return lax.ppermute(value, AXES, [(i, i ^ bit) for i in range(total)])


def all_days(block, count, place, stride):
    pieces = [block] + [swap(block, step * stride) for step in range(1, count)]
    stack = jnp.stack(pieces)
    order = place ^ jnp.arange(count)
    return stack[order].reshape((-1,) + block.shape[1:])


def sum_all(value):
    total = lax.axis_size("tm") * lax.axis_size("pts")
    low = lax.axis_index("pts") % 2
    half = value.shape[0] // 2
    kept = lax.dynamic_slice_in_dim(value, low * half, half, 0)
    sent = lax.dynamic_slice_in_dim(value, (1 - low) * half, half, 0)
    part = kept + swap(sent, 1)
    bit = 2
    while bit < total:
        part = part + swap(part, bit)
        bit *= 2
    other = swap(part, 1)
    return jnp.where(low == 0, jnp.concatenate([part, other], 0), jnp.concatenate([other, part], 0))


def on_device(precip, thresholds, bin_index, test_matrix):
    highest = lax.Precision.HIGHEST
    tm_count = lax.axis_size("tm")
    tm_place = lax.axis_index("tm")
    days_local, points_local = precip.shape
    own_rows = points_local // tm_count
    days_total = days_local * tm_count
    points_total = points_local * lax.axis_size("pts")
    full_table = harmonic_table(jnp.arange(days_total, dtype=jnp.int32))
    normal = jnp.dot(full_table, full_table.T, precision=highest)
    normal_low = jnp.linalg.cholesky(normal)
    one_hot = (
        bin_index[:, None] == jnp.arange(thresholds.shape[0], dtype=jnp.int32)[None, :]
    ).astype(jnp.float32)
    level_local = jnp.dot(one_hot, thresholds, precision=highest)
    series = lax.all_to_all(precip, "tm", split_axis=1, concat_axis=0, tiled=True)
    projections = jnp.dot(full_table, series, precision=highest)
    coefficients = normal_solve(normal_low, projections)
    anomaly = series - lax.dot_general(
        full_table, coefficients, (((0,), (0,)), ((), ())), precision=highest
    )
    level_own = lax.dynamic_slice_in_dim(level_local, tm_place * own_rows, own_rows, 0)
    excess = jnp.maximum(anomaly - level_own[None, :], 0.0)
    sketch = lax.dot_general(
        excess,
        all_days(test_matrix, tm_count, tm_place, lax.axis_size("pts")),
        (((0,), (0,)), ((), ())),
        precision=highest,
    )
    local_cross = jnp.dot(sketch.T, sketch, precision=highest)
    cross = sum_all(local_cross) / points_total
    lower = jnp.linalg.cholesky(cross)
    basis = lax.linalg.triangular_solve(
        lower, sketch, left_side=False, lower=True, transpose_a=True
    )
    return (basis, lower.T)


def solution(mesh):
    in_specs = (P("tm", "pts"), P(), P("pts"), P("tm", None))
    out_specs = (P(("pts", "tm"), None), P())
    return jax.shard_map(
        on_device, mesh=mesh, in_specs=in_specs, out_specs=out_specs, check_vma=False
    )
```

profile of v0, /device:TPU:0, one launch (start us, length us, event | category | flops | bytes accessed | tf_op | source)
XLA Modules:
  0.0 123.8 jit_solution(3260924505696430201)
XLA Ops:
  0.6 2.5 %copy.18 = f32[256,1024]{0,1:T(8,128)} copy(f32[256,1024]{1,0:T(8,128)} %param.4) | data formatting | bytes 2097152 | tf_op args[0]
  3.2 4.4 %all-to-all-start = ((f32[256,2,512]{0,2,1:T(8,128)}), f32[256,2,512]{0,2,1:T(8,128)S(1)}, u32[]{:S(2)}, u32[]{:S(2)}) async-start(f32[256,2,512]{0,2,1:T(8,128)} %bitcast), calls=%async_computation | async-start | bytes 2097152 | tf_op jit(solution)/shard_map/all_to_all | solution.py:73
  7.6 2.4 %collective-permute-start = (f32[256,256]{1,0:T(8,128)S(1)}, f32[256,256]{1,0:T(8,128)S(1)}, u32[]{:S(2)}, u32[]{:S(2)}) collective-permute-start(f32[256,256]{1,0:T(8,128)S(1)} %copy-done.1), channel_id=1, source_target_pairs={{0,16},{1,17},{2,18},{3,19},{4,20},{5,21},{6,22},{7,23},{8,24},{9,... | collective-permute-start | bytes 786440 | tf_op jit(solution)/shard_map/ppermute | solution.py:33
  10.7 0.2 fusion.40
  10.9 0.1 copy.20
  11.0 1.5 %cholesky.60 = f32[17,17]{1,0:T(8,128)S(1)} custom-call(f32[17,17]{1,0:T(8,128)S(1)} %fusion.20), custom_call_target="Cholesky" | custom-call | tf_op jit(solution)/shard_map/jit(cholesky)/cholesky | solution.py:68
  12.6 0.6 compare_reduce_fusion.2
  13.2 0.7 fusion.15
  13.9 0.4 fusion.2
  14.4 1.3 %custom-call.22 = f32[1,17,17]{1,2,0:T(8,128)S(1)} custom-call(f32[1,17,17]{2,1,0:T(8,128)S(1)} %fusion.15), custom_call_target="InvertDiagBlocksLowerTriangular" | custom-call | tf_op jit(solution)/shard_map/triangular_solve | solution.py:23
  15.8 11.8 %collective-permute-done = f32[256,256]{1,0:T(8,128)S(1)} collective-permute-done((f32[256,256]{1,0:T(8,128)S(1)}, f32[256,256]{1,0:T(8,128)S(1)}, u32[]{:S(2)}, u32[]{:S(2)}) %collective-permute-start) | collective-permute-done | bytes 262176 | tf_op jit(solution)/shard_map/ppermute | solution.py:33
  27.7 0.6 gather_fusion
  28.3 0.3 copy.19
  28.6 0.6 fusion.41
  29.2 0.2 fusion.18
  29.5 0.2 fusion.16
  29.7 1.1 fusion.1
  30.8 1.8 %fusion.42 = f32[512,256]{1,0:T(8,128)S(1)} fusion(f32[512,512]{1,0:T(8,128)S(1)} %fusion.1, f32[512,256]{1,0:T(8,128)S(1)} %bitcast.71), kind=kOutput, calls=%fused_computation.85 | convolution fusion | flops 805306368 | bytes 2097152 | tf_op jit(solution)/shard_map/dot_general | solution.py:81
  32.6 1.0 fusion.43
  33.8 1.3 %collective-permute-done.1 = f32[128,256]{0,1:T(8,128)S(1)} collective-permute-done((f32[128,256]{0,1:T(8,128)S(1)}, f32[128,256]{0,1:T(8,128)S(1)}, u32[]{:S(2)}, u32[]{:S(2)}) %collective-permute-start.1) | collective-permute-done | bytes 131104 | tf_op jit(solution)/shard_map/ppermute | solution.py:33
  35.1 1.8 %collective-permute-start.2 = (f32[128,256]{0,1:T(8,128)S(1)}, f32[128,256]{0,1:T(8,128)S(1)}, u32[]{:S(2)}, u32[]{:S(2)}) collective-permute-start(f32[128,256]{0,1:T(8,128)S(1)} %dynamic-slice_add_fusion), channel_id=1, source_target_pairs={{0,2},{1,3},{2,0},{3,1},{4,6},{5,7},{6,4},{7,5},{8,10},{9,11},{10,... | collective-permute-start | bytes 393224 | tf_op jit(solution)/shard_map/ppermute | solution.py:33
  36.9 3.8 %collective-permute-done.2 = f32[128,256]{0,1:T(8,128)S(1)} collective-permute-done((f32[128,256]{0,1:T(8,128)S(1)}, f32[128,256]{0,1:T(8,128)S(1)}, u32[]{:S(2)}, u32[]{:S(2)}) %collective-permute-start.2) | collective-permute-done | bytes 131104 | tf_op jit(solution)/shard_map/ppermute | solution.py:33
  40.7 1.9 %collective-permute-start.3 = (f32[128,256]{0,1:T(8,128)S(1)}, f32[128,256]{0,1:T(8,128)S(1)}, u32[]{:S(2)}, u32[]{:S(2)}) collective-permute-start(f32[128,256]{0,1:T(8,128)S(1)} %add.80), channel_id=1, source_target_pairs={{0,4},{1,5},{2,6},{3,7},{4,0},{5,1},{6,2},{7,3},{8,12},{9,13},{10,... | collective-permute-start | bytes 393224 | tf_op jit(solution)/shard_map/ppermute | solution.py:33
  42.6 3.2 %collective-permute-done.3 = f32[128,256]{0,1:T(8,128)S(1)} collective-permute-done((f32[128,256]{0,1:T(8,128)S(1)}, f32[128,256]{0,1:T(8,128)S(1)}, u32[]{:S(2)}, u32[]{:S(2)}) %collective-permute-start.3) | collective-permute-done | bytes 131104 | tf_op jit(solution)/shard_map/ppermute | solution.py:33
  45.8 2.9 %collective-permute-start.4 = (f32[128,256]{0,1:T(8,128)S(1)}, f32[128,256]{0,1:T(8,128)S(1)}, u32[]{:S(2)}, u32[]{:S(2)}) collective-permute-start(f32[128,256]{0,1:T(8,128)S(1)} %add.81), channel_id=1, source_target_pairs={{0,8},{1,9},{2,10},{3,11},{4,12},{5,13},{6,14},{7,15},{8,0},{9,1},... | collective-permute-start | bytes 393224 | tf_op jit(solution)/shard_map/ppermute | solution.py:33
  48.7 4.6 %collective-permute-done.4 = f32[128,256]{0,1:T(8,128)S(1)} collective-permute-done((f32[128,256]{0,1:T(8,128)S(1)}, f32[128,256]{0,1:T(8,128)S(1)}, u32[]{:S(2)}, u32[]{:S(2)}) %collective-permute-start.4) | collective-permute-done | bytes 131104 | tf_op jit(solution)/shard_map/ppermute | solution.py:33
  53.3 0.7 collective-permute-start.5
  54.0 4.3 %collective-permute-done.5 = f32[128,256]{0,1:T(8,128)S(1)} collective-permute-done((f32[128,256]{0,1:T(8,128)S(1)}, f32[128,256]{0,1:T(8,128)S(1)}, u32[]{:S(2)}, u32[]{:S(2)}) %collective-permute-start.5) | collective-permute-done | bytes 131104 | tf_op jit(solution)/shard_map/ppermute | solution.py:33
  58.4 1.3 %collective-permute-done.6 = f32[128,256]{0,1:T(8,128)S(1)} collective-permute-done((f32[128,256]{0,1:T(8,128)S(1)}, f32[128,256]{0,1:T(8,128)S(1)}, u32[]{:S(2)}, u32[]{:S(2)}) %collective-permute-start.6) | collective-permute-done | bytes 131104 | tf_op jit(solution)/shard_map/ppermute | solution.py:33
  59.8 0.1 copy.23
  60.0 11.7 %cholesky.123 = f32[128,128]{1,0:T(8,128)S(1)} custom-call(f32[128,128]{1,0:T(8,128)S(1)} %cholesky.153), custom_call_target="Cholesky" | custom-call | tf_op jit(solution)/shard_map/jit(cholesky)/cholesky | solution.py:89
  71.8 10.0 %custom-call.23 = f32[1,128,128]{1,2,0:T(8,128)S(1)} custom-call(f32[1,128,128]{2,1,0:T(8,128)S(1)} %get-tuple-element.31), custom_call_target="InvertDiagBlocksLowerTriangular" | custom-call | tf_op jit(solution)/shard_map/jit(cholesky)/cholesky | solution.py:89
  81.7 0.2 constant_dynamic-update-slice_fusion
  81.9 0.3 convolution_subtract_fusion.2
  82.2 11.7 %cholesky.140 = f32[128,128]{1,0:T(8,128)S(1)} custom-call(f32[128,128]{1,0:T(8,128)S(1)} %convolution_subtract_fusion.2), custom_call_target="Cholesky" | custom-call | tf_op jit(solution)/shard_map/jit(cholesky)/cholesky | solution.py:89
  93.9 0.7 compare_reduce_fusion
  94.7 0.6 compare_reduce_fusion.1
  96.7 4.1 %while.1 = (s32[]{:T(128)}, f32[256,256]{1,0:T(8,128)S(1)}, s32[2,2]{1,0:T(2,128)S(1)}, f32[2,128,128]{2,1,0:T(8,128)S(1)}, s32[]{:T(128)}) while((s32[]{:T(128)}, f32[256,256]{1,0:T(8,128)S(1)}, s32[2,2]{1,0:T(2,128)S(1)}, f32[2,128,128]{2,1,0:T(8,128)S(1)}, s32[]{:T(128)}) %tuple.38), condition=%wide.while_cond, body=%wide.while_body.sunk | while | flops 2 | bytes 131181 | solution.py:90
  96.7 0.6 fusion.61
  97.3 1.4 %bitcast_dynamic-update-slice_fusion.2 = f32[2,128,128]{2,1,0:T(8,128)S(1)} fusion(f32[2,128,128]{2,1,0:T(8,128)S(1)} %get-tuple-element.87, s32[]{:T(128)} %get-tuple-element.84, f32[256,256]{1,0:T(8,128)S(1)} %get-tuple-element.90, s32[]{:T(128)} %bitcast.66, s32[]{:T(128)} %bitcast.67), kind=kLoop, calls=%fused_computation.1.clone.1 | loop fusion | bytes 131084 | tf_op jit(solution)/shard_map/triangular_solve
  98.8 0.6 fusion.61
  99.4 1.4 %bitcast_dynamic-update-slice_fusion.2 = f32[2,128,128]{2,1,0:T(8,128)S(1)} fusion(f32[2,128,128]{2,1,0:T(8,128)S(1)} %get-tuple-element.87, s32[]{:T(128)} %get-tuple-element.84, f32[256,256]{1,0:T(8,128)S(1)} %get-tuple-element.90, s32[]{:T(128)} %bitcast.66, s32[]{:T(128)} %bitcast.67), kind=kLoop, calls=%fused_computation.1.clone.1 | loop fusion | bytes 131084 | tf_op jit(solution)/shard_map/triangular_solve
  100.8 19.7 %custom-call.24 = f32[2,128,128]{1,2,0:T(8,128)S(1)} custom-call(f32[2,128,128]{2,1,0:T(8,128)S(1)} %get-tuple-element.9), custom_call_target="InvertDiagBlocksLowerTriangular" | custom-call | tf_op jit(solution)/shard_map/triangular_solve | solution.py:90
  120.5 0.4 fusion.3
  120.9 0.6 convolution_subtract_fusion.1
  121.5 0.4 fusion.10
  122.0 1.0 copy.24
  123.0 0.8 copy.25
  (44 shorter events, 1.5 us)
Async XLA Ops:
  0.6 13.3 %copy-start = (f32[64]{0:T(128)S(1)}, f32[64]{0:T(128)}, u32[]{:S(2)}) copy-start(f32[64]{0:T(128)} %param.5) | copy-start | bytes 772
  3.2 4.4 %copy-start.1 = (f32[256,256]{1,0:T(8,128)S(1)}, f32[256,256]{1,0:T(8,128)}, u32[]{:S(2)}) copy-start(f32[256,256]{1,0:T(8,128)} %param.7) | copy-start | bytes 786436
  3.2 25.1 %all-to-all-start = ((f32[256,2,512]{0,2,1:T(8,128)}), f32[256,2,512]{0,2,1:T(8,128)S(1)}, u32[]{:S(2)}, u32[]{:S(2)}) async-start(f32[256,2,512]{0,2,1:T(8,128)} %bitcast), calls=%async_computation | async-start | bytes 2097152 | tf_op jit(solution)/shard_map/all_to_all | solution.py:73
  7.6 20.0 %collective-permute-start = (f32[256,256]{1,0:T(8,128)S(1)}, f32[256,256]{1,0:T(8,128)S(1)}, u32[]{:S(2)}, u32[]{:S(2)}) collective-permute-start(f32[256,256]{1,0:T(8,128)S(1)} %copy-done.1), channel_id=1, source_target_pairs={{0,16},{1,17},{2,18},{3,19},{4,20},{5,21},{6,22},{7,23},{8,24},{9,... | collective-permute-start | bytes 786440 | tf_op jit(solution)/shard_map/ppermute | solution.py:33
  13.2 0.7 copy-start.2
  33.7 1.4 %collective-permute-start.1 = (f32[128,256]{0,1:T(8,128)S(1)}, f32[128,256]{0,1:T(8,128)S(1)}, u32[]{:S(2)}, u32[]{:S(2)}) collective-permute-start(f32[128,256]{0,1:T(8,128)S(1)} %constant_dynamic-slice_fusion.1), channel_id=1, source_target_pairs={{0,1},{1,0},{2,3},{3,2},{4,5},{5,4},{6,7},{7,6},{8,9},{9,8},{10,11... | collective-permute-start | bytes 393224 | tf_op jit(solution)/shard_map/ppermute | solution.py:33
  35.1 5.6 %collective-permute-start.2 = (f32[128,256]{0,1:T(8,128)S(1)}, f32[128,256]{0,1:T(8,128)S(1)}, u32[]{:S(2)}, u32[]{:S(2)}) collective-permute-start(f32[128,256]{0,1:T(8,128)S(1)} %dynamic-slice_add_fusion), channel_id=1, source_target_pairs={{0,2},{1,3},{2,0},{3,1},{4,6},{5,7},{6,4},{7,5},{8,10},{9,11},{10,... | collective-permute-start | bytes 393224 | tf_op jit(solution)/shard_map/ppermute | solution.py:33
  40.7 5.0 %collective-permute-start.3 = (f32[128,256]{0,1:T(8,128)S(1)}, f32[128,256]{0,1:T(8,128)S(1)}, u32[]{:S(2)}, u32[]{:S(2)}) collective-permute-start(f32[128,256]{0,1:T(8,128)S(1)} %add.80), channel_id=1, source_target_pairs={{0,4},{1,5},{2,6},{3,7},{4,0},{5,1},{6,2},{7,3},{8,12},{9,13},{10,... | collective-permute-start | bytes 393224 | tf_op jit(solution)/shard_map/ppermute | solution.py:33
  45.8 7.5 %collective-permute-start.4 = (f32[128,256]{0,1:T(8,128)S(1)}, f32[128,256]{0,1:T(8,128)S(1)}, u32[]{:S(2)}, u32[]{:S(2)}) collective-permute-start(f32[128,256]{0,1:T(8,128)S(1)} %add.81), channel_id=1, source_target_pairs={{0,8},{1,9},{2,10},{3,11},{4,12},{5,13},{6,14},{7,15},{8,0},{9,1},... | collective-permute-start | bytes 393224 | tf_op jit(solution)/shard_map/ppermute | solution.py:33
  53.3 5.0 %collective-permute-start.5 = (f32[128,256]{0,1:T(8,128)S(1)}, f32[128,256]{0,1:T(8,128)S(1)}, u32[]{:S(2)}, u32[]{:S(2)}) collective-permute-start(f32[128,256]{0,1:T(8,128)S(1)} %add.82), channel_id=1, source_target_pairs={{0,16},{1,17},{2,18},{3,19},{4,20},{5,21},{6,22},{7,23},{8,24},{9,... | collective-permute-start | bytes 393224 | tf_op jit(solution)/shard_map/ppermute | solution.py:33
  58.3 1.4 %collective-permute-start.6 = (f32[128,256]{0,1:T(8,128)S(1)}, f32[128,256]{0,1:T(8,128)S(1)}, u32[]{:S(2)}, u32[]{:S(2)}) collective-permute-start(f32[128,256]{0,1:T(8,128)S(1)} %add.83), channel_id=1, source_target_pairs={{0,1},{1,0},{2,3},{3,2},{4,5},{5,4},{6,7},{7,6},{8,9},{9,8},{10,11... | collective-permute-start | bytes 393224 | tf_op jit(solution)/shard_map/ppermute | solution.py:33
where the time goes:
time: 124 us
  other arithmetic  59.6 us (48%)
  waiting for transfers between devices  30.4 us (25%)
  starting transfers between devices  14.2 us (11%)
  local copies, waits for them, and re-layouts  9.85 us (8%)
  matrix products  7.48 us (6%)
  between operations  2.3 us (2%)
    another operation x7, other arithmetic, on_device(): lower = jnp.linalg.cholesky(cross)  34.8 us
    ppermute x7, waiting for transfers between devices, swap(): return lax.ppermute(value, AXES, [(i, i ^ bit) for i in range(total)])  30.4 us
    another operation x3, other arithmetic, on_device(): lax.linalg.triangular_solve(lower, sketch, left_side=False, lower=True, t...  19.7 us
    ppermute x7, starting transfers between devices, swap(): return lax.ppermute(value, AXES, [(i, i ^ bit) for i in range(total)])  9.77 us
    all_to_all x1, starting transfers between devices, on_device(): lax.all_to_all(precip, 'tm', split_axis=1, concat_axis=0, tiled=True)  4.39 us
    unnamed x9, local copies, waits for them, and re-layouts  4.38 us
    another operation x6, local copies, waits for them, and re-layouts  4.02 us
  transfers between devices with their start and end apart: 8, of which 7 were waited for; matrix products, arithmetic and copies ran while one was open for 5% of the time, Pallas kernels for 0%

commit v1 on v0

--- a/solution.py
+++ b/solution.py
@@ -6,6 +6,13 @@
 
 HARM = 8
 year_days = 365.25
+
+
+def exchange_blocks(block, name, split, join):
+    count = lax.axis_size(name)
+    blocks = jnp.stack(jnp.split(block, count, axis=split), axis=0)
+    blocks = lax.all_to_all(blocks, name, split_axis=0, concat_axis=0)
+    return jnp.concatenate(blocks, axis=join)
 
 
 def harmonic_table(day_number):
@@ -70,7 +77,7 @@
         bin_index[:, None] == jnp.arange(thresholds.shape[0], dtype=jnp.int32)[None, :]
     ).astype(jnp.float32)
     level_local = jnp.dot(one_hot, thresholds, precision=highest)
-    series = lax.all_to_all(precip, "tm", split_axis=1, concat_axis=0, tiled=True)
+    series = exchange_blocks(precip, "tm", 1, 0)
     projections = jnp.dot(full_table, series, precision=highest)
     coefficients = normal_solve(normal_low, projections)
     anomaly = series - lax.dot_general(

time: 124 us -> 123 us (level)
  local copies, waits for them, and re-layouts: 9.85 us -> 8.15 us
    unnamed x9 -> x8, local copies, waits for them, and re-layouts: 4.38 us -> 1.85 us
    another operation x6 -> x7, local copies, waits for them, and re-layouts: 4.02 us -> 5.19 us
where the time goes in v1:
time: 123 us
  other arithmetic  60.6 us (49%)
  waiting for transfers between devices  30.4 us (25%)
  starting transfers between devices  14.2 us (12%)
  local copies, waits for them, and re-layouts  8.15 us (7%)
  matrix products  7.48 us (6%)
  between operations  2.24 us (2%)
    another operation x7, other arithmetic, on_device(): lower = jnp.linalg.cholesky(cross)  34.8 us
    ppermute x7, waiting for transfers between devices, swap(): return lax.ppermute(value, AXES, [(i, i ^ bit) for i in range(total)])  30.4 us
    another operation x3, other arithmetic, on_device(): lax.linalg.triangular_solve(lower, sketch, left_side=False, lower=True, t...  19.7 us
    ppermute x7, starting transfers between devices, swap(): return lax.ppermute(value, AXES, [(i, i ^ bit) for i in range(total)])  9.77 us
    all_to_all x1, starting transfers between devices, exchange_blocks(): blocks = lax.all_to_all(blocks, name, split_axis=0, concat_axis=0)  4.39 us
    another operation x6, local copies, waits for them, and re-layouts  3.91 us
  transfers between devices with their start and end apart: 8, of which 7 were waited for; matrix products, arithmetic and copies ran while one was open for 5% of the time, Pallas kernels for 0%

profile of v1, /device:TPU:0, one launch (start us, length us, event | category | flops | bytes accessed | tf_op | source)
XLA Modules:
  0.0 123.0 jit_solution(13583939784859081679)
XLA Ops:
  0.6 1.3 %slice_bitcast_fusion.1 = (f32[1,256,512]{2,1,0:T(8,128)S(1)}, f32[1,256,512]{2,1,0:T(8,128)S(1)}) fusion(f32[256,1024]{1,0:T(8,128)} %param.4), kind=kLoop, calls=%fused_computation.13 | loop fusion | bytes 2097152 | tf_op jit(solution)/shard_map/stack | solution.py:13
  1.9 1.0 pad_maximum_fusion
  3.0 4.4 %all-to-all-start = ((f32[2,256,512]{2,1,0:T(8,128)}), f32[2,256,512]{2,1,0:T(8,128)S(1)}, u32[]{:S(2)}, u32[]{:S(2)}) async-start(f32[2,256,512]{2,1,0:T(8,128)} %pad_maximum_fusion), calls=%async_computation | async-start | bytes 2097152 | tf_op jit(solution)/shard_map/all_to_all | solution.py:14
  7.4 2.4 %collective-permute-start = (f32[256,256]{1,0:T(8,128)S(1)}, f32[256,256]{1,0:T(8,128)S(1)}, u32[]{:S(2)}, u32[]{:S(2)}) collective-permute-start(f32[256,256]{1,0:T(8,128)S(1)} %copy-done.1), channel_id=1, source_target_pairs={{0,16},{1,17},{2,18},{3,19},{4,20},{5,21},{6,22},{7,23},{8,24},{9,... | collective-permute-start | bytes 786440 | tf_op jit(solution)/shard_map/ppermute | solution.py:40
  10.5 0.2 fusion.40
  10.7 0.1 copy.6
  10.8 1.5 %cholesky.60 = f32[17,17]{1,0:T(8,128)S(1)} custom-call(f32[17,17]{1,0:T(8,128)S(1)} %fusion.20), custom_call_target="Cholesky" | custom-call | tf_op jit(solution)/shard_map/jit(cholesky)/cholesky | solution.py:75
  12.4 0.6 compare_reduce_fusion.2
  13.0 0.7 fusion.15
  13.7 0.4 fusion.2
  14.2 1.3 %custom-call.22 = f32[1,17,17]{1,2,0:T(8,128)S(1)} custom-call(f32[1,17,17]{2,1,0:T(8,128)S(1)} %fusion.15), custom_call_target="InvertDiagBlocksLowerTriangular" | custom-call | tf_op jit(solution)/shard_map/triangular_solve | solution.py:30
  15.6 11.8 %collective-permute-done = f32[256,256]{1,0:T(8,128)S(1)} collective-permute-done((f32[256,256]{1,0:T(8,128)S(1)}, f32[256,256]{1,0:T(8,128)S(1)}, u32[]{:S(2)}, u32[]{:S(2)}) %collective-permute-start) | collective-permute-done | bytes 262176 | tf_op jit(solution)/shard_map/ppermute | solution.py:40
  27.4 0.6 gather_fusion
  28.0 0.6 fusion.41
  28.7 0.2 fusion.18
  28.9 0.2 fusion.16
  29.1 1.1 fusion.1
  30.2 1.8 %fusion.42 = f32[512,256]{1,0:T(8,128)S(1)} fusion(f32[512,512]{1,0:T(8,128)S(1)} %fusion.1, f32[512,256]{1,0:T(8,128)S(1)} %bitcast.72), kind=kOutput, calls=%fused_computation.88 | convolution fusion | flops 805306368 | bytes 2097152 | tf_op jit(solution)/shard_map/dot_general | solution.py:88
  32.0 1.0 fusion.43
  33.2 1.3 %collective-permute-done.1 = f32[128,256]{0,1:T(8,128)S(1)} collective-permute-done((f32[128,256]{0,1:T(8,128)S(1)}, f32[128,256]{0,1:T(8,128)S(1)}, u32[]{:S(2)}, u32[]{:S(2)}) %collective-permute-start.1) | collective-permute-done | bytes 131104 | tf_op jit(solution)/shard_map/ppermute | solution.py:40
  34.5 1.8 %collective-permute-start.2 = (f32[128,256]{0,1:T(8,128)S(1)}, f32[128,256]{0,1:T(8,128)S(1)}, u32[]{:S(2)}, u32[]{:S(2)}) collective-permute-start(f32[128,256]{0,1:T(8,128)S(1)} %dynamic-slice_add_fusion), channel_id=1, source_target_pairs={{0,2},{1,3},{2,0},{3,1},{4,6},{5,7},{6,4},{7,5},{8,10},{9,11},{10,... | collective-permute-start | bytes 393224 | tf_op jit(solution)/shard_map/ppermute | solution.py:40
  36.3 3.8 %collective-permute-done.2 = f32[128,256]{0,1:T(8,128)S(1)} collective-permute-done((f32[128,256]{0,1:T(8,128)S(1)}, f32[128,256]{0,1:T(8,128)S(1)}, u32[]{:S(2)}, u32[]{:S(2)}) %collective-permute-start.2) | collective-permute-done | bytes 131104 | tf_op jit(solution)/shard_map/ppermute | solution.py:40
  40.2 1.9 %collective-permute-start.3 = (f32[128,256]{0,1:T(8,128)S(1)}, f32[128,256]{0,1:T(8,128)S(1)}, u32[]{:S(2)}, u32[]{:S(2)}) collective-permute-start(f32[128,256]{0,1:T(8,128)S(1)} %add.80), channel_id=1, source_target_pairs={{0,4},{1,5},{2,6},{3,7},{4,0},{5,1},{6,2},{7,3},{8,12},{9,13},{10,... | collective-permute-start | bytes 393224 | tf_op jit(solution)/shard_map/ppermute | solution.py:40
  42.0 3.2 %collective-permute-done.3 = f32[128,256]{0,1:T(8,128)S(1)} collective-permute-done((f32[128,256]{0,1:T(8,128)S(1)}, f32[128,256]{0,1:T(8,128)S(1)}, u32[]{:S(2)}, u32[]{:S(2)}) %collective-permute-start.3) | collective-permute-done | bytes 131104 | tf_op jit(solution)/shard_map/ppermute | solution.py:40
  45.2 2.9 %collective-permute-start.4 = (f32[128,256]{0,1:T(8,128)S(1)}, f32[128,256]{0,1:T(8,128)S(1)}, u32[]{:S(2)}, u32[]{:S(2)}) collective-permute-start(f32[128,256]{0,1:T(8,128)S(1)} %add.81), channel_id=1, source_target_pairs={{0,8},{1,9},{2,10},{3,11},{4,12},{5,13},{6,14},{7,15},{8,0},{9,1},... | collective-permute-start | bytes 393224 | tf_op jit(solution)/shard_map/ppermute | solution.py:40
  48.1 4.6 %collective-permute-done.4 = f32[128,256]{0,1:T(8,128)S(1)} collective-permute-done((f32[128,256]{0,1:T(8,128)S(1)}, f32[128,256]{0,1:T(8,128)S(1)}, u32[]{:S(2)}, u32[]{:S(2)}) %collective-permute-start.4) | collective-permute-done | bytes 131104 | tf_op jit(solution)/shard_map/ppermute | solution.py:40
  52.7 0.7 collective-permute-start.5
  53.5 4.3 %collective-permute-done.5 = f32[128,256]{0,1:T(8,128)S(1)} collective-permute-done((f32[128,256]{0,1:T(8,128)S(1)}, f32[128,256]{0,1:T(8,128)S(1)}, u32[]{:S(2)}, u32[]{:S(2)}) %collective-permute-start.5) | collective-permute-done | bytes 131104 | tf_op jit(solution)/shard_map/ppermute | solution.py:40
  57.9 1.3 %collective-permute-done.6 = f32[128,256]{0,1:T(8,128)S(1)} collective-permute-done((f32[128,256]{0,1:T(8,128)S(1)}, f32[128,256]{0,1:T(8,128)S(1)}, u32[]{:S(2)}, u32[]{:S(2)}) %collective-permute-start.6) | collective-permute-done | bytes 131104 | tf_op jit(solution)/shard_map/ppermute | solution.py:40
  59.2 0.1 copy.9
  59.4 11.7 %cholesky.123 = f32[128,128]{1,0:T(8,128)S(1)} custom-call(f32[128,128]{1,0:T(8,128)S(1)} %cholesky.153), custom_call_target="Cholesky" | custom-call | tf_op jit(solution)/shard_map/jit(cholesky)/cholesky | solution.py:96
  71.2 10.0 %custom-call.23 = f32[1,128,128]{1,2,0:T(8,128)S(1)} custom-call(f32[1,128,128]{2,1,0:T(8,128)S(1)} %get-tuple-element.29), custom_call_target="InvertDiagBlocksLowerTriangular" | custom-call | tf_op jit(solution)/shard_map/jit(cholesky)/cholesky | solution.py:96
  81.2 0.2 constant_dynamic-update-slice_fusion
  81.4 0.3 convolution_subtract_fusion.2
  81.6 11.7 %cholesky.140 = f32[128,128]{1,0:T(8,128)S(1)} custom-call(f32[128,128]{1,0:T(8,128)S(1)} %convolution_subtract_fusion.2), custom_call_target="Cholesky" | custom-call | tf_op jit(solution)/shard_map/jit(cholesky)/cholesky | solution.py:96
  93.4 0.7 compare_reduce_fusion
  94.1 0.6 compare_reduce_fusion.1
  96.1 3.9 %while.1 = (s32[]{:T(128)}, f32[256,256]{1,0:T(8,128)S(1)}, s32[2,2]{1,0:T(2,128)S(1)}, f32[2,128,128]{2,1,0:T(8,128)S(1)}, s32[]{:T(128)}) while((s32[]{:T(128)}, f32[256,256]{1,0:T(8,128)S(1)}, s32[2,2]{1,0:T(2,128)S(1)}, f32[2,128,128]{2,1,0:T(8,128)S(1)}, s32[]{:T(128)}) %tuple.37), condition=%wide.while_cond, body=%wide.while_body.sunk | while | flops 2 | bytes 131181 | solution.py:97
  96.1 0.6 fusion.61
  96.7 1.4 %bitcast_dynamic-update-slice_fusion.2 = f32[2,128,128]{2,1,0:T(8,128)S(1)} fusion(f32[2,128,128]{2,1,0:T(8,128)S(1)} %get-tuple-element.85, s32[]{:T(128)} %get-tuple-element.82, f32[256,256]{1,0:T(8,128)S(1)} %get-tuple-element.88, s32[]{:T(128)} %bitcast.68, s32[]{:T(128)} %bitcast.69), kind=kLoop, calls=%fused_computation.1.clone.1 | loop fusion | bytes 131084 | tf_op jit(solution)/shard_map/triangular_solve
  98.1 0.6 fusion.61
  98.7 1.4 %bitcast_dynamic-update-slice_fusion.2 = f32[2,128,128]{2,1,0:T(8,128)S(1)} fusion(f32[2,128,128]{2,1,0:T(8,128)S(1)} %get-tuple-element.85, s32[]{:T(128)} %get-tuple-element.82, f32[256,256]{1,0:T(8,128)S(1)} %get-tuple-element.88, s32[]{:T(128)} %bitcast.68, s32[]{:T(128)} %bitcast.69), kind=kLoop, calls=%fused_computation.1.clone.1 | loop fusion | bytes 131084 | tf_op jit(solution)/shard_map/triangular_solve
  100.1 19.7 %custom-call.24 = f32[2,128,128]{1,2,0:T(8,128)S(1)} custom-call(f32[2,128,128]{2,1,0:T(8,128)S(1)} %get-tuple-element.9), custom_call_target="InvertDiagBlocksLowerTriangular" | custom-call | tf_op jit(solution)/shard_map/triangular_solve | solution.py:97
  119.7 0.4 fusion.3
  120.2 0.6 convolution_subtract_fusion.1
  120.7 0.4 fusion.10
  121.2 1.0 copy.10
  122.2 0.8 copy.11
  (44 shorter events, 1.5 us)
Async XLA Ops:
  0.6 13.1 %copy-start = (f32[64]{0:T(128)S(1)}, f32[64]{0:T(128)}, u32[]{:S(2)}) copy-start(f32[64]{0:T(128)} %param.5) | copy-start | bytes 772
  3.0 4.4 %copy-start.1 = (f32[256,256]{1,0:T(8,128)S(1)}, f32[256,256]{1,0:T(8,128)}, u32[]{:S(2)}) copy-start(f32[256,256]{1,0:T(8,128)} %param.7) | copy-start | bytes 786436
  3.0 25.1 %all-to-all-start = ((f32[2,256,512]{2,1,0:T(8,128)}), f32[2,256,512]{2,1,0:T(8,128)S(1)}, u32[]{:S(2)}, u32[]{:S(2)}) async-start(f32[2,256,512]{2,1,0:T(8,128)} %pad_maximum_fusion), calls=%async_computation | async-start | bytes 2097152 | tf_op jit(solution)/shard_map/all_to_all | solution.py:14
  7.4 20.0 %collective-permute-start = (f32[256,256]{1,0:T(8,128)S(1)}, f32[256,256]{1,0:T(8,128)S(1)}, u32[]{:S(2)}, u32[]{:S(2)}) collective-permute-start(f32[256,256]{1,0:T(8,128)S(1)} %copy-done.1), channel_id=1, source_target_pairs={{0,16},{1,17},{2,18},{3,19},{4,20},{5,21},{6,22},{7,23},{8,24},{9,... | collective-permute-start | bytes 786440 | tf_op jit(solution)/shard_map/ppermute | solution.py:40
  13.0 0.7 copy-start.2
  33.1 1.4 %collective-permute-start.1 = (f32[128,256]{0,1:T(8,128)S(1)}, f32[128,256]{0,1:T(8,128)S(1)}, u32[]{:S(2)}, u32[]{:S(2)}) collective-permute-start(f32[128,256]{0,1:T(8,128)S(1)} %constant_dynamic-slice_fusion.1), channel_id=1, source_target_pairs={{0,1},{1,0},{2,3},{3,2},{4,5},{5,4},{6,7},{7,6},{8,9},{9,8},{10,11... | collective-permute-start | bytes 393224 | tf_op jit(solution)/shard_map/ppermute | solution.py:40
  34.5 5.6 %collective-permute-start.2 = (f32[128,256]{0,1:T(8,128)S(1)}, f32[128,256]{0,1:T(8,128)S(1)}, u32[]{:S(2)}, u32[]{:S(2)}) collective-permute-start(f32[128,256]{0,1:T(8,128)S(1)} %dynamic-slice_add_fusion), channel_id=1, source_target_pairs={{0,2},{1,3},{2,0},{3,1},{4,6},{5,7},{6,4},{7,5},{8,10},{9,11},{10,... | collective-permute-start | bytes 393224 | tf_op jit(solution)/shard_map/ppermute | solution.py:40
  40.2 5.0 %collective-permute-start.3 = (f32[128,256]{0,1:T(8,128)S(1)}, f32[128,256]{0,1:T(8,128)S(1)}, u32[]{:S(2)}, u32[]{:S(2)}) collective-permute-start(f32[128,256]{0,1:T(8,128)S(1)} %add.80), channel_id=1, source_target_pairs={{0,4},{1,5},{2,6},{3,7},{4,0},{5,1},{6,2},{7,3},{8,12},{9,13},{10,... | collective-permute-start | bytes 393224 | tf_op jit(solution)/shard_map/ppermute | solution.py:40
  45.2 7.5 %collective-permute-start.4 = (f32[128,256]{0,1:T(8,128)S(1)}, f32[128,256]{0,1:T(8,128)S(1)}, u32[]{:S(2)}, u32[]{:S(2)}) collective-permute-start(f32[128,256]{0,1:T(8,128)S(1)} %add.81), channel_id=1, source_target_pairs={{0,8},{1,9},{2,10},{3,11},{4,12},{5,13},{6,14},{7,15},{8,0},{9,1},... | collective-permute-start | bytes 393224 | tf_op jit(solution)/shard_map/ppermute | solution.py:40
  52.7 5.0 %collective-permute-start.5 = (f32[128,256]{0,1:T(8,128)S(1)}, f32[128,256]{0,1:T(8,128)S(1)}, u32[]{:S(2)}, u32[]{:S(2)}) collective-permute-start(f32[128,256]{0,1:T(8,128)S(1)} %add.82), channel_id=1, source_target_pairs={{0,16},{1,17},{2,18},{3,19},{4,20},{5,21},{6,22},{7,23},{8,24},{9,... | collective-permute-start | bytes 393224 | tf_op jit(solution)/shard_map/ppermute | solution.py:40
  57.8 1.4 %collective-permute-start.6 = (f32[128,256]{0,1:T(8,128)S(1)}, f32[128,256]{0,1:T(8,128)S(1)}, u32[]{:S(2)}, u32[]{:S(2)}) collective-permute-start(f32[128,256]{0,1:T(8,128)S(1)} %add.83), channel_id=1, source_target_pairs={{0,1},{1,0},{2,3},{3,2},{4,5},{5,4},{6,7},{7,6},{8,9},{9,8},{10,11... | collective-permute-start | bytes 393224 | tf_op jit(solution)/shard_map/ppermute | solution.py:40
